TPU v7x, 32 devices: a whole 2x2x4 slice. The times are simulated.
32 devices in a mesh: groups: 2 (over y), seq: 4 (over z), head: 4 (over x, core).
Axes of the slice: x: 2, y: 2, z: 4, core: 2. Of those that a mesh axis runs over, the one named last changes fastest.
Arguments:
- queries: bfloat16 [4096, 2048], P(('groups', 'seq'), 'head'), parts along dimension 0, may hold values from -8 to 8
- keys: bfloat16 [4096, 2048], P(('groups', 'seq'), 'head'), parts along dimension 0, may hold values from -8 to 8
- values: bfloat16 [4096, 2048], P(('groups', 'seq'), 'head'), parts along dimension 0, may hold values from -12 to 12
- w_out: bfloat16 [2048, 2048], replicated, may hold values from -0.125 to 0.125
Outputs:
- projected: bfloat16 [4096, 2048], P(('groups', 'seq', 'head')), parts along dimension 0
There are 2 independent parts, one for each index of `groups`. A program takes and returns all parts, laid end to end along the dimension named above; an argument that names none is the same for every part. Nothing has to cross between parts.
All inputs are finite; a program needn't handle non-finite values.
Results may differ from a plain program's by a relative error of at most 0.005.
Values may be sent and summed in bfloat16 or wider, within the bound.
A program may use at most 128 MiB of HBM per device.

v0:
```python
import math
import jax
import jax.numpy as jnp
from jax import lax
from jax.sharding import PartitionSpec as P

HD = 128
WINDOW = 2048


def shifted(value, axis, steps):
    count = lax.axis_size(axis)
    first, last = (max(0, -steps), min(count, count - steps))
    return lax.ppermute(value, axis, [(source, source + steps) for source in range(first, last)])


def per_device(queries, keys, values, w_out):
    length_dev, width = queries.shape
    heads_dev = width // HD
    block_rows = min(512, length_dev)
    block_count = length_dev // block_rows
    highest = lax.Precision.HIGHEST
    seq_index = lax.axis_index("seq")
    q_blocks = queries.reshape(block_count, block_rows, heads_dev, HD)
    k_blocks = keys.reshape(block_count, block_rows, heads_dev, HD)
    v_blocks = values.reshape(block_count, block_rows, heads_dev, HD)
    block_states = jnp.einsum(
        "bkhd,bkhe->bhde", k_blocks, v_blocks, preferred_element_type=jnp.float32
    )
    own_state = jnp.sum(block_states, axis=0)
    earlier = jnp.cumsum(block_states, axis=0) - block_states
    piece = lax.all_gather(own_state[None], "seq", axis=0, tiled=True)
    order = jnp.arange(piece.shape[0], dtype=jnp.int32)
    keep = order < seq_index
    prefix = jnp.sum(jnp.where(keep[:, None, None, None], piece, 0.0), axis=0)
    causal = jnp.arange(block_rows)[:, None] >= jnp.arange(block_rows)[None, :]
    local_scores = jnp.einsum(
        "bqhd,bkhd->bhqk", q_blocks, k_blocks, preferred_element_type=jnp.float32
    )
    local_scores = jnp.where(causal, local_scores, 0.0)
    intra = jnp.einsum(
        "bhqk,bkhe->bqhe", local_scores, v_blocks.astype(jnp.float32), precision=highest
    )
    state_before = prefix[None] + earlier
    inter = jnp.einsum(
        "bqhd,bhde->bqhe", q_blocks.astype(jnp.float32), state_before, precision=highest
    )
    linear = (intra + inter).reshape(length_dev, heads_dev, HD)
    normed = linear / jnp.sqrt(jnp.mean(linear * linear, axis=-1, keepdims=True) + 1e-06)
    reach = min(WINDOW // length_dev, lax.axis_size("seq") - 1)
    received = [shifted((keys, values), "seq", distance) for distance in range(1, reach + 1)]
    pad_rows = WINDOW - reach * length_dev
    filler = jnp.zeros((pad_rows, width), keys.dtype)
    wide_keys = jnp.concatenate([filler] + [pair[0] for pair in reversed(received)] + [keys], 0)
    wide_values = jnp.concatenate([filler] + [pair[1] for pair in reversed(received)] + [values], 0)
    wide_keys = wide_keys.reshape(-1, heads_dev, HD)
    wide_values = wide_values.reshape(-1, heads_dev, HD)
    scale = 1.0 / math.sqrt(HD)
    span = WINDOW + block_rows
    query_pos = jnp.arange(block_rows, dtype=jnp.int32)[:, None]
    key_pos = jnp.arange(span, dtype=jnp.int32)[None, :]
    band = (key_pos > query_pos) & (key_pos <= query_pos + WINDOW)
    rows_q = queries.reshape(block_rows, heads_dev, HD)
    anchor = seq_index * length_dev + 0 - WINDOW
    valid = band & (anchor + key_pos >= 0)
    scores = (
        jnp.einsum("qhd,khd->hqk", rows_q, wide_keys, preferred_element_type=jnp.float32) * scale
    )
    scores = jnp.where(valid[None], scores, -1e30)
    top = jnp.max(scores, axis=-1, keepdims=True)
    expo = jnp.where(valid[None], jnp.exp(scores - top), 0.0)
    total = jnp.sum(expo, axis=-1)
    weights = expo.astype(jnp.bfloat16)
    summed = jnp.einsum("hqk,khe->qhe", weights, wide_values, preferred_element_type=jnp.float32)
    pieces = summed / jnp.transpose(total)[:, :, None]
    mixed = (normed + pieces).astype(jnp.bfloat16).reshape(length_dev, width)
    head_count = lax.axis_size("head")
    share = length_dev // head_count
    grouped = mixed.reshape(head_count, share, width)
    return jnp.dot(
        lax.all_to_all(grouped, "head", split_axis=0, concat_axis=2, tiled=True)[0],
        w_out,
        preferred_element_type=jnp.float32,
    ).astype(jnp.bfloat16)


def solution(mesh):
    return jax.shard_map(
        per_device,
        mesh=mesh,
        in_specs=(
            P(("groups", "seq"), "head"),
            P(("groups", "seq"), "head"),
            P(("groups", "seq"), "head"),
            P(),
        ),
        out_specs=P(("groups", "seq", "head"), None),
        check_vma=False,
    )
```

profile of v0, /device:TPU:16, one launch (start us, length us, event | category | flops | bytes accessed | tf_op | source)
XLA Modules:
  0.0 174.5 jit_solution(8869428141898482623)
XLA Ops:
  6.5 1.3 copy.52
  7.9 1.5 collective-permute-start.3
  9.3 1.3 collective-permute-start.4
  10.6 3.3 %collective-permute-start.5 = (bf16[512,512]{0,1:T(8,128)(2,1)S(1)}, bf16[512,512]{0,1:T(8,128)(2,1)}, u32[]{:S(2)}, u32[]{:S(2)}) collective-permute-start(bf16[512,512]{0,1:T(8,128)(2,1)S(1)} %copy.52), channel_id=1, source_target_pairs={{0,4},{4,8},{8,12},{1,5},{5,9},{9,13},{2,6},{6,10},{10,14},{3,7},{... | collective-permute-start | bytes 1572872 | tf_op jit(solution)/shard_map/ppermute | solution.py:14
  13.9 1.3 copy.37
  15.2 1.5 collective-permute-start
  16.7 1.3 collective-permute-start.1
  18.0 2.0 %fusion.37 = f32[4,128,128]{2,1,0:T(8,128)} fusion(bf16[512,4,128]{0,2,1:T(8,128)(2,1)S(1)} %bitcast.96, bf16[512,512]{1,0:T(8,128)(2,1)} %param.6), kind=kOutput, calls=%fused_computation.30 | convolution fusion | flops 67108864 | bytes 1310720 | tf_op jit(solution)/shard_map/bkhd,bkhe->bhde/dot_general | solution.py:27
  20.0 0.0 all-gather.3.cloned.1.call-update
  20.1 1.9 %fusion.8 = pred[512,2560]{0,1:T(8,128)(4,1)S(1)} fusion(s32[512]{0:T(512)S(1)} %iota_add_fusion, pred[2560]{0:T(1024)(128)(4,1)S(1)} %add_compare_fusion), kind=kLoop, calls=%fused_computation.12 | loop fusion | flops 5242880 | bytes 1315328 | tf_op jit(solution)/shard_map/and | solution.py:65
  22.0 2.8 %fusion.46 = f32[4,512,512]{2,1,0:T(8,128)} fusion(bf16[512,4,128]{0,2,1:T(8,128)(2,1)S(1)} %bitcast.97, bf16[512,512]{1,0:T(8,128)(2,1)S(1)} %copy-done), kind=kOutput, calls=%fused_computation.37 | convolution fusion | flops 268435456 | bytes 5242880 | tf_op jit(solution)/shard_map/bqhd,bkhd->bhqk/dot_general | solution.py:37
  24.8 0.1 iota_compare_fusion.2
  24.9 0.0 collective-permute-done.3
  24.9 5.3 %collective-permute-start.2 = (bf16[512,512]{0,1:T(8,128)(2,1)S(1)}, bf16[512,512]{0,1:T(8,128)(2,1)S(1)}, u32[]{:S(2)}, u32[]{:S(2)}) collective-permute-start(bf16[512,512]{0,1:T(8,128)(2,1)S(1)} %copy.37), channel_id=1, source_target_pairs={{0,4},{4,8},{8,12},{1,5},{5,9},{9,13},{2,6},{6,10},{10,14},{3,7},{... | collective-permute-start | bytes 1572872 | tf_op jit(solution)/shard_map/ppermute | solution.py:14
  30.2 1.1 constant_dynamic-update-slice_fusion.7
  31.3 10.9 %collective-permute-done.4 = bf16[512,512]{0,1:T(8,128)(2,1)} collective-permute-done((bf16[512,512]{0,1:T(8,128)(2,1)S(1)}, bf16[512,512]{0,1:T(8,128)(2,1)}, u32[]{:S(2)}, u32[]{:S(2)}) %collective-permute-start.4) | collective-permute-done | bytes 524320 | tf_op jit(solution)/shard_map/ppermute | solution.py:14
  42.2 1.1 constant_dynamic-update-slice_fusion.6
  43.3 55.3 %collective-permute-done.5 = bf16[512,512]{0,1:T(8,128)(2,1)} collective-permute-done((bf16[512,512]{0,1:T(8,128)(2,1)S(1)}, bf16[512,512]{0,1:T(8,128)(2,1)}, u32[]{:S(2)}, u32[]{:S(2)}) %collective-permute-start.5) | collective-permute-done | bytes 524320 | tf_op jit(solution)/shard_map/ppermute | solution.py:14
  98.6 1.1 constant_dynamic-update-slice_fusion.5
  99.7 1.5 constant_dynamic-update-slice_fusion.3
  101.2 1.1 constant_dynamic-update-slice_fusion.2
  102.3 18.6 %collective-permute-done.2 = bf16[512,512]{0,1:T(8,128)(2,1)S(1)} collective-permute-done((bf16[512,512]{0,1:T(8,128)(2,1)S(1)}, bf16[512,512]{0,1:T(8,128)(2,1)S(1)}, u32[]{:S(2)}, u32[]{:S(2)}) %collective-permute-start.2) | collective-permute-done | bytes 524320 | tf_op jit(solution)/shard_map/ppermute | solution.py:14
  121.0 1.4 copy-done.3
  122.4 15.3 %fusion.63 = (f32[4,512]{1,0:T(4,128)S(1)}, bf16[4,512,2560]{1,2,0:T(8,128)(2,1)}) fusion(pred[512,2560]{0,1:T(8,128)(4,1)S(1)} %fusion.8, bf16[2560,4,128]{0,2,1:T(8,128)(2,1)} %bitcast.101, bf16[512,512]{1,0:T(8,128)(2,1)S(1)} %copy-done), kind=kOutput, calls=%fused_computation.64 | convolution fusion | flops 1373637120 | bytes 14950400 | tf_op jit(solution)/shard_map/sub | solution.py:71
  137.7 1.4 select_reduce_fusion
  139.2 0.6 fusion.44
  139.8 5.2 %multiply_reduce_fusion = (f32[512,4]{0,1:T(4,128)S(1)}, f32[512,4,128]{0,2,1:T(8,128)S(1)}) fusion(f32[4,128,512]{2,1,0:T(8,128)S(1)} %fusion.44, f32[4,512,512]{2,1,0:T(8,128)} %fusion.46, pred[512,512]{1,0:T(8,128)(4,1)S(1)} %iota_compare_fusion.2, bf16[512,512]{1,0:T(8,128)(2,1)S(1)} %copy-done.1), kind=kOutput, calls=%fused_computation.26 | convolution fusion | flops 1612445696 | bytes 7086080 | tf_op jit(solution)/shard_map/bhqk,bkhe->bqhe/dot_general | solution.py:41
  145.0 5.6 %fusion.33 = bf16[512,4,128]{0,2,1:T(8,128)(2,1)S(1)} fusion(bf16[2560,4,128]{0,2,1:T(8,128)(2,1)S(1)} %bitcast.100, bf16[4,512,2560]{1,2,0:T(8,128)(2,1)} %get-tuple-element.6, f32[512,4,128]{0,2,1:T(8,128)S(1)} %get-tuple-element.8, f32[512,4]{0,1:T(4,128)S(1)} %bitcast.102, f32[512,4]{0,1:T(4,128)S(1)} %add_sqrt_fusion), kind=kOutput, calls=%fused_computation.25 | convolution fusion | flops 1343225856 | bytes 14696448 | tf_op jit(solution)/shard_map/hqk,khe->qhe/dot_general | solution.py:74
  150.6 0.1 reshape_reshape.3
  150.7 0.1 copy.48
  150.8 11.4 %all_to_all.15 = bf16[4,128,512]{1,2,0:T(8,128)(2,1)S(1)} all-to-all(bf16[4,128,512]{1,2,0:T(8,128)(2,1)S(1)} %copy.48), channel_id=1, replica_groups=mesh['groups'=2,'seq'=4,'head'=4] {'head'}, dimensions={0} | all-to-all | bytes 1048576 | tf_op jit(solution)/shard_map/all_to_all | solution.py:81
  162.2 5.5 %convolution_convert_fusion = bf16[128,2048]{1,0:T(8,128)(2,1)} fusion(bf16[128,2048]{0,1:T(8,128)(2,1)S(1)} %bitcast.98, bf16[2048,2048]{1,0:T(8,128)(2,1)} %param.7), kind=kOutput, calls=%fused_computation.15 | convolution fusion | flops 1074003968 | bytes 9437184 | tf_op jit(solution)/shard_map/dot_general | solution.py:80
  (24 shorter events, 0.2 us)
Async XLA Ops:
  6.5 15.4 %copy-start = (bf16[512,512]{1,0:T(8,128)(2,1)S(1)}, bf16[512,512]{1,0:T(8,128)(2,1)}, u32[]{:S(2)}) copy-start(bf16[512,512]{1,0:T(8,128)(2,1)} %param.4) | copy-start | bytes 1572868
  6.5 131.2 %all-gather.3.cloned.1.call-start = ((), (), s32[]{:S(2)}) async-start(), calls=%async_computation.1 | async-start | bytes 1310720 | tf_op jit(solution)/shard_map/all_gather | solution.py:32
  7.9 17.1 %collective-permute-start.3 = (bf16[512,512]{0,1:T(8,128)(2,1)S(1)}, bf16[512,512]{0,1:T(8,128)(2,1)}, u32[]{:S(2)}, u32[]{:S(2)}) collective-permute-start(bf16[512,512]{0,1:T(8,128)(2,1)S(1)} %copy.52), channel_id=1, source_target_pairs={{0,12},{1,13},{2,14},{3,15},{16,28},{17,29},{18,30},{19,31}} | collective-permute-start | bytes 1572872 | tf_op jit(solution)/shard_map/ppermute | solution.py:14
  9.3 32.9 %collective-permute-start.4 = (bf16[512,512]{0,1:T(8,128)(2,1)S(1)}, bf16[512,512]{0,1:T(8,128)(2,1)}, u32[]{:S(2)}, u32[]{:S(2)}) collective-permute-start(bf16[512,512]{0,1:T(8,128)(2,1)S(1)} %copy.52), channel_id=1, source_target_pairs={{0,8},{4,12},{1,9},{5,13},{2,10},{6,14},{3,11},{7,15},{16,24},{20,... | collective-permute-start | bytes 1572872 | tf_op jit(solution)/shard_map/ppermute | solution.py:14
  10.6 88.0 %collective-permute-start.5 = (bf16[512,512]{0,1:T(8,128)(2,1)S(1)}, bf16[512,512]{0,1:T(8,128)(2,1)}, u32[]{:S(2)}, u32[]{:S(2)}) collective-permute-start(bf16[512,512]{0,1:T(8,128)(2,1)S(1)} %copy.52), channel_id=1, source_target_pairs={{0,4},{4,8},{8,12},{1,5},{5,9},{9,13},{2,6},{6,10},{10,14},{3,7},{... | collective-permute-start | bytes 1572872 | tf_op jit(solution)/shard_map/ppermute | solution.py:14
  15.2 84.5 %collective-permute-start = (bf16[512,512]{0,1:T(8,128)(2,1)S(1)}, bf16[512,512]{0,1:T(8,128)(2,1)}, u32[]{:S(2)}, u32[]{:S(2)}) collective-permute-start(bf16[512,512]{0,1:T(8,128)(2,1)S(1)} %copy.37), channel_id=1, source_target_pairs={{0,12},{1,13},{2,14},{3,15},{16,28},{17,29},{18,30},{19,31}} | collective-permute-start | bytes 1572872 | tf_op jit(solution)/shard_map/ppermute | solution.py:14
  16.7 84.5 %collective-permute-start.1 = (bf16[512,512]{0,1:T(8,128)(2,1)S(1)}, bf16[512,512]{0,1:T(8,128)(2,1)}, u32[]{:S(2)}, u32[]{:S(2)}) collective-permute-start(bf16[512,512]{0,1:T(8,128)(2,1)S(1)} %copy.37), channel_id=1, source_target_pairs={{0,8},{4,12},{1,9},{5,13},{2,10},{6,14},{3,11},{7,15},{16,24},{20,... | collective-permute-start | bytes 1572872 | tf_op jit(solution)/shard_map/ppermute | solution.py:14
  24.9 95.9 %collective-permute-start.2 = (bf16[512,512]{0,1:T(8,128)(2,1)S(1)}, bf16[512,512]{0,1:T(8,128)(2,1)S(1)}, u32[]{:S(2)}, u32[]{:S(2)}) collective-permute-start(bf16[512,512]{0,1:T(8,128)(2,1)S(1)} %copy.37), channel_id=1, source_target_pairs={{0,4},{4,8},{8,12},{1,5},{5,9},{9,13},{2,6},{6,10},{10,14},{3,7},{... | collective-permute-start | bytes 1572872 | tf_op jit(solution)/shard_map/ppermute | solution.py:14
  99.7 21.2 %copy-start.5 = (bf16[2560,512]{0,1:T(8,128)(2,1)}, bf16[2560,512]{0,1:T(8,128)(2,1)S(1)}, u32[]{:S(2)}) copy-start(bf16[2560,512]{0,1:T(8,128)(2,1)S(1)} %constant_dynamic-update-slice_fusion.4) | copy-start | bytes 7864324
  121.0 1.5 copy-start.3
  122.4 16.8 %copy-start.2 = (f32[4,128,128]{2,1,0:T(8,128)S(1)}, f32[4,128,128]{2,1,0:T(8,128)}, u32[]{:S(2)}) copy-start(f32[4,128,128]{2,1,0:T(8,128)} %fusion.37) | copy-start | bytes 786436
  137.7 2.1 %copy-start.1 = (bf16[512,512]{1,0:T(8,128)(2,1)S(1)}, bf16[512,512]{1,0:T(8,128)(2,1)}, u32[]{:S(2)}) copy-start(bf16[512,512]{1,0:T(8,128)(2,1)} %param.6) | copy-start | bytes 1572868
  139.8 5.2 %copy-start.4 = (bf16[2560,512]{0,1:T(8,128)(2,1)S(1)}, bf16[2560,512]{0,1:T(8,128)(2,1)}, u32[]{:S(2)}) copy-start(bf16[2560,512]{0,1:T(8,128)(2,1)} %copy-done.3) | copy-start | bytes 7864324
Sparse Core Ops, SparseCore 0:
  20.2 60.3 all-gather.2
where the time goes:
time: 175 us; the launch traced here: 174 us
  waiting for transfers between devices  84.8 us (48%)
  matrix products  36.9 us (21%)
  starting transfers between devices  14.2 us (8%)
  between operations  13.7 us (8%)
  blocking collectives  11.4 us (7%)
  local copies, waits for them, and re-layouts  10.2 us (6%)
  other arithmetic  3.42 us (2%)
    ppermute x6, waiting for transfers between devices, shifted(): lax.ppermute(value, axis, [(source, source + steps) for source in range(f...  84.7 us
    sub x1, matrix products, per_device(): expo = jnp.where(valid[None], jnp.exp(scores - top), 0.0)  15.3 us
    ppermute x6, starting transfers between devices, shifted(): lax.ppermute(value, axis, [(source, source + steps) for source in range(f...  14.2 us
    all_to_all x1, blocking collectives, per_device(): lax.all_to_all(grouped, 'head', split_axis=0, concat_axis=2, tiled=True)[0]  11.4 us
    unnamed x21, local copies, waits for them, and re-layouts  8.63 us
    dot_general x1, matrix products, per_device(): jnp.einsum('hqk,khe->qhe', weights, wide_values, preferred_element_type=j...  5.56 us
    dot_general x1, matrix products, per_device(): jnp.dot(lax.all_to_all(grouped, 'head', split_axis=0, concat_axis=2, tile...  5.46 us
    dot_general x1, matrix products, per_device(): jnp.einsum('bhqk,bkhe->bqhe', local_scores, v_blocks.astype(jnp.float32),...  5.17 us
  transfers between devices with their start and end apart: 7, of which 3 were waited for; matrix products, arithmetic and copies ran while one was open for 17% of the time, Pallas kernels for 0%

commit v1 on v0

--- a/solution.py
+++ b/solution.py
@@ -78,7 +78,12 @@
     share = length_dev // head_count
     grouped = mixed.reshape(head_count, share, width)
     return jnp.dot(
-        lax.all_to_all(grouped, "head", split_axis=0, concat_axis=2, tiled=True)[0],
+        jnp.concatenate(
+            lax.all_to_all(
+                jnp.stack(jnp.split(grouped, lax.axis_size("head"), axis=0)), "head", 0, 0
+            ),
+            axis=2,
+        )[0],
         w_out,
         preferred_element_type=jnp.float32,
     ).astype(jnp.bfloat16)

time: 175 us -> 172 us (0.983)
  matrix products: 36.9 us -> 33.7 us
    dot_general x1, matrix products: 5.46 us -> 2.09 us  [per_device(): jnp.dot(jnp.concatenate(lax.all_to_all(jnp.stack(jnp.split(grouped, lax.a...]
    unnamed x21 -> x25, local copies, waits for them, and re-layouts: 8.63 us -> 8.65 us
where the time goes in v1:
time: 172 us; the launch traced here: 171 us
  waiting for transfers between devices  84.7 us (49%)
  matrix products  33.7 us (20%)
  starting transfers between devices  14.2 us (8%)
  between operations  13.7 us (8%)
  blocking collectives  11.4 us (7%)
  local copies, waits for them, and re-layouts  10.1 us (6%)
  other arithmetic  3.49 us (2%)
    ppermute x6, waiting for transfers between devices, shifted(): lax.ppermute(value, axis, [(source, source + steps) for source in range(f...  84.7 us
    sub x1, matrix products, per_device(): expo = jnp.where(valid[None], jnp.exp(scores - top), 0.0)  15.3 us
    ppermute x6, starting transfers between devices, shifted(): lax.ppermute(value, axis, [(source, source + steps) for source in range(f...  14.2 us
    all_to_all x1, blocking collectives, per_device(): lax.all_to_all(jnp.stack(jnp.split(grouped, lax.axis_size('head'), axis=0...  11.4 us
    unnamed x25, local copies, waits for them, and re-layouts  8.65 us
    dot_general x1, matrix products, per_device(): jnp.einsum('hqk,khe->qhe', weights, wide_values, preferred_element_type=j...  5.71 us
    dot_general x1, matrix products, per_device(): jnp.einsum('bhqk,bkhe->bqhe', local_scores, v_blocks.astype(jnp.float32),...  5.17 us
  transfers between devices with their start and end apart: 7, of which 3 were waited for; matrix products, arithmetic and copies ran while one was open for 17% of the time, Pallas kernels for 0%

profile of v1, /device:TPU:16, one launch (start us, length us, event | category | flops | bytes accessed | tf_op | source)
XLA Modules:
  0.0 171.3 jit_solution(7335458259961436119)
XLA Ops:
  6.5 1.3 copy.50
  7.9 1.5 collective-permute-start.3
  9.3 1.3 collective-permute-start.4
  10.6 3.3 %collective-permute-start.5 = (bf16[512,512]{0,1:T(8,128)(2,1)S(1)}, bf16[512,512]{0,1:T(8,128)(2,1)}, u32[]{:S(2)}, u32[]{:S(2)}) collective-permute-start(bf16[512,512]{0,1:T(8,128)(2,1)S(1)} %copy.50), channel_id=1, source_target_pairs={{0,4},{4,8},{8,12},{1,5},{5,9},{9,13},{2,6},{6,10},{10,14},{3,7},{... | collective-permute-start | bytes 1572872 | tf_op jit(solution)/shard_map/ppermute | solution.py:14
  13.9 1.3 copy.36
  15.2 1.5 collective-permute-start
  16.7 1.3 collective-permute-start.1
  18.0 2.0 %fusion.37 = f32[4,128,128]{2,1,0:T(8,128)} fusion(bf16[512,4,128]{0,2,1:T(8,128)(2,1)S(1)} %bitcast.98, bf16[512,512]{1,0:T(8,128)(2,1)} %param.6), kind=kOutput, calls=%fused_computation.30 | convolution fusion | flops 67108864 | bytes 1310720 | tf_op jit(solution)/shard_map/bkhd,bkhe->bhde/dot_general | solution.py:27
  20.0 0.0 all-gather.3.cloned.1.call-update
  20.1 1.9 %fusion.8 = pred[512,2560]{0,1:T(8,128)(4,1)S(1)} fusion(s32[512]{0:T(512)S(1)} %iota_add_fusion, pred[2560]{0:T(1024)(128)(4,1)S(1)} %add_compare_fusion), kind=kLoop, calls=%fused_computation.12 | loop fusion | flops 5242880 | bytes 1315328 | tf_op jit(solution)/shard_map/and | solution.py:65
  21.9 2.8 %fusion.46 = f32[4,512,512]{2,1,0:T(8,128)} fusion(bf16[512,4,128]{0,2,1:T(8,128)(2,1)S(1)} %bitcast.99, bf16[512,512]{1,0:T(8,128)(2,1)S(1)} %copy-done), kind=kOutput, calls=%fused_computation.37 | convolution fusion | flops 268435456 | bytes 5242880 | tf_op jit(solution)/shard_map/bqhd,bkhd->bhqk/dot_general | solution.py:37
  24.7 0.1 iota_compare_fusion.2
  24.9 5.3 %collective-permute-start.2 = (bf16[512,512]{0,1:T(8,128)(2,1)S(1)}, bf16[512,512]{0,1:T(8,128)(2,1)S(1)}, u32[]{:S(2)}, u32[]{:S(2)}) collective-permute-start(bf16[512,512]{0,1:T(8,128)(2,1)S(1)} %copy.36), channel_id=1, source_target_pairs={{0,4},{4,8},{8,12},{1,5},{5,9},{9,13},{2,6},{6,10},{10,14},{3,7},{... | collective-permute-start | bytes 1572872 | tf_op jit(solution)/shard_map/ppermute | solution.py:14
  30.2 1.1 constant_dynamic-update-slice_fusion.7
  31.3 10.9 %collective-permute-done.4 = bf16[512,512]{0,1:T(8,128)(2,1)} collective-permute-done((bf16[512,512]{0,1:T(8,128)(2,1)S(1)}, bf16[512,512]{0,1:T(8,128)(2,1)}, u32[]{:S(2)}, u32[]{:S(2)}) %collective-permute-start.4) | collective-permute-done | bytes 524320 | tf_op jit(solution)/shard_map/ppermute | solution.py:14
  42.2 1.1 constant_dynamic-update-slice_fusion.6
  43.3 55.3 %collective-permute-done.5 = bf16[512,512]{0,1:T(8,128)(2,1)} collective-permute-done((bf16[512,512]{0,1:T(8,128)(2,1)S(1)}, bf16[512,512]{0,1:T(8,128)(2,1)}, u32[]{:S(2)}, u32[]{:S(2)}) %collective-permute-start.5) | collective-permute-done | bytes 524320 | tf_op jit(solution)/shard_map/ppermute | solution.py:14
  98.6 1.1 constant_dynamic-update-slice_fusion.5
  99.7 1.5 constant_dynamic-update-slice_fusion.3
  101.2 1.1 constant_dynamic-update-slice_fusion.2
  102.3 18.6 %collective-permute-done.2 = bf16[512,512]{0,1:T(8,128)(2,1)S(1)} collective-permute-done((bf16[512,512]{0,1:T(8,128)(2,1)S(1)}, bf16[512,512]{0,1:T(8,128)(2,1)S(1)}, u32[]{:S(2)}, u32[]{:S(2)}) %collective-permute-start.2) | collective-permute-done | bytes 524320 | tf_op jit(solution)/shard_map/ppermute | solution.py:14
  121.0 1.5 copy-done.3
  122.4 15.3 %fusion.64 = (f32[4,512]{1,0:T(4,128)S(1)}, bf16[4,512,2560]{1,2,0:T(8,128)(2,1)}) fusion(pred[512,2560]{0,1:T(8,128)(4,1)S(1)} %fusion.8, bf16[2560,4,128]{0,2,1:T(8,128)(2,1)} %bitcast.107, bf16[512,512]{1,0:T(8,128)(2,1)S(1)} %copy-done), kind=kOutput, calls=%fused_computation.66 | convolution fusion | flops 1373637120 | bytes 14950400 | tf_op jit(solution)/shard_map/sub | solution.py:71
  137.7 1.4 select_reduce_fusion
  139.2 0.6 fusion.44
  139.8 5.2 %multiply_reduce_fusion = (f32[512,4]{0,1:T(4,128)S(1)}, f32[512,4,128]{0,2,1:T(8,128)S(1)}) fusion(f32[4,128,512]{2,1,0:T(8,128)S(1)} %fusion.44, f32[4,512,512]{2,1,0:T(8,128)} %fusion.46, pred[512,512]{1,0:T(8,128)(4,1)S(1)} %iota_compare_fusion.2, bf16[512,512]{1,0:T(8,128)(2,1)S(1)} %copy-done.1), kind=kOutput, calls=%fused_computation.26 | convolution fusion | flops 1612445696 | bytes 7086080 | tf_op jit(solution)/shard_map/bhqk,bkhe->bqhe/dot_general | solution.py:41
  145.0 0.0 slice-start
  145.0 5.7 %fusion.33 = bf16[512,4,128]{0,2,1:T(8,128)(2,1)S(1)} fusion(bf16[2560,4,128]{0,2,1:T(8,128)(2,1)S(1)} %bitcast.106, bf16[4,512,2560]{1,2,0:T(8,128)(2,1)} %get-tuple-element.10, f32[512,4,128]{0,2,1:T(8,128)S(1)} %get-tuple-element.12, f32[512,4]{0,1:T(4,128)S(1)} %bitcast.108, f32[512,4]{0,1:T(4,128)S(1)} %add_sqrt_fusion), kind=kOutput, calls=%fused_computation.25 | convolution fusion | flops 1343225856 | bytes 14696448 | tf_op jit(solution)/shard_map/hqk,khe->qhe/dot_general | solution.py:74
  150.8 0.1 fusion.63
  150.9 0.1 pad_maximum_fusion
  151.0 11.4 %all_to_all.5 = bf16[4,1,128,512]{2,3,1,0:T(8,128)(2,1)S(1)} all-to-all(bf16[4,1,128,512]{2,3,1,0:T(8,128)(2,1)S(1)} %pad_maximum_fusion), channel_id=1, replica_groups=mesh['groups'=2,'seq'=4,'head'=4] {'head'}, dimensions={0} | all-to-all | bytes 1048576 | tf_op jit(solution)/shard_map/all_to_all | solution.py:82
  162.4 2.1 %convolution_convert_fusion = bf16[128,2048]{1,0:T(8,128)(2,1)} fusion(bf16[128,2048]{0,1:T(8,128)(2,1)S(1)} %bitcast.100, bf16[2048,2048]{1,0:T(8,128)(2,1)S(1)} %bitcast.97), kind=kOutput, calls=%fused_computation.15 | convolution fusion | flops 1074003968 | bytes 9437184 | tf_op jit(solution)/shard_map/dot_general | solution.py:80
  (29 shorter events, 0.2 us)
Async XLA Ops:
  6.5 15.4 %copy-start = (bf16[512,512]{1,0:T(8,128)(2,1)S(1)}, bf16[512,512]{1,0:T(8,128)(2,1)}, u32[]{:S(2)}) copy-start(bf16[512,512]{1,0:T(8,128)(2,1)} %param.4) | copy-start | bytes 1572868
  6.5 131.2 %all-gather.3.cloned.1.call-start = ((), (), s32[]{:S(2)}) async-start(), calls=%async_computation.1 | async-start | bytes 1310720 | tf_op jit(solution)/shard_map/all_gather | solution.py:32
  7.9 17.0 %collective-permute-start.3 = (bf16[512,512]{0,1:T(8,128)(2,1)S(1)}, bf16[512,512]{0,1:T(8,128)(2,1)}, u32[]{:S(2)}, u32[]{:S(2)}) collective-permute-start(bf16[512,512]{0,1:T(8,128)(2,1)S(1)} %copy.50), channel_id=1, source_target_pairs={{0,12},{1,13},{2,14},{3,15},{16,28},{17,29},{18,30},{19,31}} | collective-permute-start | bytes 1572872 | tf_op jit(solution)/shard_map/ppermute | solution.py:14
  9.3 32.9 %collective-permute-start.4 = (bf16[512,512]{0,1:T(8,128)(2,1)S(1)}, bf16[512,512]{0,1:T(8,128)(2,1)}, u32[]{:S(2)}, u32[]{:S(2)}) collective-permute-start(bf16[512,512]{0,1:T(8,128)(2,1)S(1)} %copy.50), channel_id=1, source_target_pairs={{0,8},{4,12},{1,9},{5,13},{2,10},{6,14},{3,11},{7,15},{16,24},{20,... | collective-permute-start | bytes 1572872 | tf_op jit(solution)/shard_map/ppermute | solution.py:14
  10.6 88.0 %collective-permute-start.5 = (bf16[512,512]{0,1:T(8,128)(2,1)S(1)}, bf16[512,512]{0,1:T(8,128)(2,1)}, u32[]{:S(2)}, u32[]{:S(2)}) collective-permute-start(bf16[512,512]{0,1:T(8,128)(2,1)S(1)} %copy.50), channel_id=1, source_target_pairs={{0,4},{4,8},{8,12},{1,5},{5,9},{9,13},{2,6},{6,10},{10,14},{3,7},{... | collective-permute-start | bytes 1572872 | tf_op jit(solution)/shard_map/ppermute | solution.py:14
  15.2 84.5 %collective-permute-start = (bf16[512,512]{0,1:T(8,128)(2,1)S(1)}, bf16[512,512]{0,1:T(8,128)(2,1)}, u32[]{:S(2)}, u32[]{:S(2)}) collective-permute-start(bf16[512,512]{0,1:T(8,128)(2,1)S(1)} %copy.36), channel_id=1, source_target_pairs={{0,12},{1,13},{2,14},{3,15},{16,28},{17,29},{18,30},{19,31}} | collective-permute-start | bytes 1572872 | tf_op jit(solution)/shard_map/ppermute | solution.py:14
  16.7 84.5 %collective-permute-start.1 = (bf16[512,512]{0,1:T(8,128)(2,1)S(1)}, bf16[512,512]{0,1:T(8,128)(2,1)}, u32[]{:S(2)}, u32[]{:S(2)}) collective-permute-start(bf16[512,512]{0,1:T(8,128)(2,1)S(1)} %copy.36), channel_id=1, source_target_pairs={{0,8},{4,12},{1,9},{5,13},{2,10},{6,14},{3,11},{7,15},{16,24},{20,... | collective-permute-start | bytes 1572872 | tf_op jit(solution)/shard_map/ppermute | solution.py:14
  24.9 96.0 %collective-permute-start.2 = (bf16[512,512]{0,1:T(8,128)(2,1)S(1)}, bf16[512,512]{0,1:T(8,128)(2,1)S(1)}, u32[]{:S(2)}, u32[]{:S(2)}) collective-permute-start(bf16[512,512]{0,1:T(8,128)(2,1)S(1)} %copy.36), channel_id=1, source_target_pairs={{0,4},{4,8},{8,12},{1,5},{5,9},{9,13},{2,6},{6,10},{10,14},{3,7},{... | collective-permute-start | bytes 1572872 | tf_op jit(solution)/shard_map/ppermute | solution.py:14
  99.7 21.2 %copy-start.5 = (bf16[2560,512]{0,1:T(8,128)(2,1)}, bf16[2560,512]{0,1:T(8,128)(2,1)S(1)}, u32[]{:S(2)}) copy-start(bf16[2560,512]{0,1:T(8,128)(2,1)S(1)} %constant_dynamic-update-slice_fusion.4) | copy-start | bytes 7864324
  121.0 1.5 copy-start.3
  122.4 16.7 %copy-start.2 = (f32[4,128,128]{2,1,0:T(8,128)S(1)}, f32[4,128,128]{2,1,0:T(8,128)}, u32[]{:S(2)}) copy-start(f32[4,128,128]{2,1,0:T(8,128)} %fusion.37) | copy-start | bytes 786436
  137.7 2.1 %copy-start.1 = (bf16[512,512]{1,0:T(8,128)(2,1)S(1)}, bf16[512,512]{1,0:T(8,128)(2,1)}, u32[]{:S(2)}) copy-start(bf16[512,512]{1,0:T(8,128)(2,1)} %param.6) | copy-start | bytes 1572868
  139.8 5.2 %copy-start.4 = (bf16[2560,512]{0,1:T(8,128)(2,1)S(1)}, bf16[2560,512]{0,1:T(8,128)(2,1)}, u32[]{:S(2)}) copy-start(bf16[2560,512]{0,1:T(8,128)(2,1)} %copy-done.3) | copy-start | bytes 7864324
  145.0 17.4 %slice-start = ((s8[8388608]{0:T(1024)(128)(4,1)}), s8[4194304]{0:T(1024)(128)(4,1)S(1)}, s32[]{:S(2)}) async-start(s8[8388608]{0:T(1024)(128)(4,1)} %bitcast.96), calls=%async_computation.2 | async-start | bytes 8388608
  145.0 17.3 %slice-start.1 = ((s8[8388608]{0:T(1024)(128)(4,1)}), s8[4194304]{0:T(1024)(128)(4,1)S(1)}, s32[]{:S(2)}) async-start(s8[8388608]{0:T(1024)(128)(4,1)} %bitcast.96), calls=%async_computation.3 | async-start | bytes 8388608
Sparse Core Ops, SparseCore 0:
  20.2 60.3 all-gather.2
